TPU v7x, 32 devices: a whole 2x2x4 slice. The times are simulated.
32 devices in a mesh: grp: 4 (over z), mem: 8 (over y, x, core).
Axes of the slice: x: 2, y: 2, z: 4, core: 2. Of those that a mesh axis runs over, the one named last changes fastest.
Arguments:
- bin_sketch: bfloat16 [256, 1024], P(('grp', 'mem')), may hold values from -6 to 6
- rep_sketch: bfloat16 [8192, 1024], P(('grp', 'mem')), may hold values from -6 to 6
- bin_profile: bfloat16 [256, 32768], P('grp', 'mem'), may hold values from -6 to 6
- member_profile: bfloat16 [12, 256, 32768], P('grp', None, 'mem'), may hold values from -6 to 6
- bin_routes: int32 [256, 2], P('grp'), may hold values from 0 to 11, all different within a row; in each aligned block of 64 rows (0 to 63, 64 to 127, ...) at most 16 rows name the same one
- owner_slot: int32 [12], replicated, may hold values from 0 to 11, each once
- cluster_sizes: int32 [12], replicated, may hold values from 128 to 256, as said below
Outputs:
- coarse_scores: bfloat16 [256, 8192], P(None, ('grp', 'mem'))
- fine_scores: float32 [256, 2, 256], P('grp', None, 'mem')
Inputs may be any that keep to these rules, and one draw needn't show every extreme that they name: `bin_routes`: within the bins of one index of grp (64 consecutive bins), no cluster is named by more than 16 routes, a bound that some block reaches; the two clusters of a bin differ. `owner_slot`: A permutation. `cluster_sizes`: each a multiple of 128.
All inputs are finite; a program needn't handle non-finite values.
Results may differ from a plain program's by a relative error of at most 0.001.
Values may be sent and summed in bfloat16 or wider, within the bound.
No kernel may reach another device: no remote copies, remote signals or barrier semaphores. Data moves between devices by JAX's collectives and lax.ppermute only.
A program may use at most 128 MiB of HBM per device.

v0:
```python
import jax
import jax.numpy as jnp
from jax import lax
from jax.sharding import PartitionSpec as P

FW = 32768
MOST = 16


def local(
    bin_sketch, rep_sketch, bin_profile, member_profile, bin_routes, owner_slot, cluster_sizes
):
    coarse_scale = bin_sketch.shape[1] ** (-0.5)
    group_rows = lax.all_gather(bin_sketch, "mem", axis=0, tiled=True)
    product = lax.dot_general(
        lax.all_gather(group_rows, "grp", axis=0, tiled=True),
        rep_sketch,
        (((1,), (1,)), ((), ())),
        preferred_element_type=jnp.float32,
    )
    coarse_scores = (product * coarse_scale).astype(jnp.bfloat16)
    rows_here, width_here = bin_profile.shape
    slot_count, members, _ = member_profile.shape
    groups = lax.axis_size("grp")
    cluster_total = owner_slot.shape[0]
    capacity = groups * slot_count * MOST
    route_flat = bin_routes.reshape(-1)
    cluster_ids = jnp.arange(cluster_total, dtype=jnp.int32)
    route_hit = (route_flat[:, None] == cluster_ids[None, :]).astype(jnp.int32)
    storage = jnp.sum(route_hit * owner_slot[None, :], axis=1)
    route_size = jnp.sum(route_hit * cluster_sizes[None, :], axis=1)
    route_rank = jnp.sum((jnp.cumsum(route_hit, axis=0) - route_hit) * route_hit, axis=1)
    slot_index = storage * MOST + route_rank
    source = bin_profile[jnp.arange(route_flat.shape[0], dtype=jnp.int32) // 2]
    outgoing = jnp.zeros((capacity, width_here), jnp.bfloat16).at[slot_index].set(source)
    outgoing = outgoing.reshape(groups, slot_count * MOST, width_here)
    incoming = lax.all_to_all(outgoing, "grp", split_axis=0, concat_axis=0, tiled=True)
    incoming = incoming.reshape(groups, slot_count, MOST, width_here)
    partial_value = jnp.einsum(
        "gsmc,sjc->gsmj", incoming, member_profile, preferred_element_type=jnp.float32
    )
    summed = lax.psum_scatter(partial_value, "mem", scatter_dimension=3, tiled=True)
    returned = lax.all_to_all(summed, "grp", split_axis=0, concat_axis=0, tiled=True)
    member_local = returned.shape[3]
    route_scores = returned.reshape(capacity, member_local)[slot_index] * FW ** (-0.5)
    column = lax.axis_index("mem") * member_local + jnp.arange(member_local, dtype=jnp.int32)
    member_live = column[None, :] < route_size[:, None]
    fine_scores = jnp.where(member_live, route_scores, 0.0).reshape(rows_here, 2, member_local)
    return (coarse_scores, fine_scores)


def solution(mesh):
    return jax.shard_map(
        local,
        mesh=mesh,
        in_specs=(
            P(("grp", "mem"), None),
            P(("grp", "mem"), None),
            P("grp", "mem"),
            P("grp", None, "mem"),
            P("grp", None),
            P(),
            P(),
        ),
        out_specs=(P(None, ("grp", "mem")), P("grp", None, "mem")),
        check_vma=False,
    )
```

profile of v0, /device:TPU:0, one launch (start us, length us, event | category | flops | bytes accessed | tf_op | source)
XLA Modules:
  0.0 133.0 jit_solution(8496143700417119367)
XLA Ops:
  7.2 0.0 copy-start
  7.2 0.8 copy.17
  8.0 0.1 eq.15
  8.2 0.1 fusion.12
  8.3 0.2 reduce_window_sum.11
  8.4 0.9 select_reduce_fusion.2
  9.3 0.0 copy-done
  9.3 6.4 %scatter_custom_fusion = bf16[192,4096]{1,0:T(8,128)(2,1)} fusion(s32[128]{0:T(128)S(1)} %fusion.14, bf16[64,4096]{1,0:T(8,128)(2,1)S(1)} %copy-done, s32[1024]{0:T(1024)S(1)} %pad_clamp_fusion.1, bf16[]{:T(256)} %constant.36.clone.1), kind=kCustom, calls=%fused_computation.9 | custom fusion | bytes 1572866 | tf_op jit(solution)/shard_map/scatter | solution.py:35
  15.7 0.0 copy-start.2
  15.7 6.5 %all-to-all-start = ((bf16[4,48,4096]{2,1,0:T(8,128)(2,1)}), bf16[4,48,4096]{2,1,0:T(8,128)(2,1)S(1)}, u32[]{:S(2)}, u32[]{:S(2)}) async-start(bf16[4,48,4096]{2,1,0:T(8,128)(2,1)} %bitcast.3), calls=%async_computation | async-start | bytes 3145728 | tf_op jit(solution)/shard_map/all_to_all | solution.py:37
  22.2 0.0 reduce-scatter.4.cloned.1.call-start
  22.2 0.0 copy-done.2
  22.2 9.2 %all_gather.6 = bf16[64,1024]{1,0:T(8,128)(2,1)S(1)} all-gather(bf16[8,1024]{1,0:T(8,128)(2,1)S(1)} %copy-done.2), channel_id=1, replica_groups=mesh['grp'=4,'mem'=8] {'mem'}, dimensions={0}, use_global_device_ids=true | all-gather | bytes 147456 | tf_op jit(solution)/shard_map/all_gather | solution.py:14
  31.4 38.1 %all_gather.7 = bf16[256,1024]{1,0:T(8,128)(2,1)S(1)} all-gather(bf16[64,1024]{1,0:T(8,128)(2,1)S(1)} %all_gather.6), channel_id=1, replica_groups=mesh['grp'=4,'mem'=8] {'grp'}, dimensions={0}, use_global_device_ids=true | all-gather | bytes 655360 | tf_op jit(solution)/shard_map/all_gather | solution.py:16
  69.5 0.0 all-to-all-done
  69.5 4.8 %fusion.4 = f32[4,3,16,256]{3,2,0,1:T(8,128)S(1)} fusion(bf16[3,256,4096]{2,1,0:T(8,128)(2,1)} %param.10, bf16[4,3,16,4096]{3,2,1,0:T(8,128)(2,1)S(1)} %bitcast.25), kind=kOutput, calls=%fused_computation.8 | convolution fusion | flops 402653184 | bytes 8060928 | tf_op jit(solution)/shard_map/gsmc,sjc->gsmj/dot_general | solution.py:39
  74.4 0.0 copy-start.1
  74.4 0.7 copy.23
  75.1 1.5 %reshape.132 = f32[256,192]{1,0:T(8,128)} reshape(f32[256,3,4,16]{3,2,1,0:T(4,128)S(1)} %bitcast.24) | data formatting | bytes 393216
  76.6 0.0 reduce-scatter.4.cloned.1.call-update
  76.6 0.0 copy-done.1
  76.6 1.0 fusion.3
  77.6 33.7 %reduce-scatter.4.cloned.1.call-done = f32[32,192]{1,0:T(8,128)} async-done(((f32[256,192]{1,0:T(8,128)}), f32[32,192]{1,0:T(8,128)}) %reduce-scatter.4.cloned.1.call-update) | async-done | bytes 24592
  111.4 0.9 reshape.133
  112.3 0.1 copy.20
  112.4 0.7 reshape.140
  113.1 4.6 %all-to-all-start.1 = ((f32[4,1,1536]{2,1,0:T(1,128)}), f32[4,1,1536]{2,1,0:T(1,128)S(1)}, u32[]{:S(2)}, u32[]{:S(2)}) async-start(f32[4,1,1536]{2,1,0:T(1,128)} %reshape.140), calls=%async_computation.1 | async-start | bytes 49152 | tf_op jit(solution)/shard_map/all_to_all | solution.py:43
  117.7 0.1 lt.38
  117.9 0.1 copy.18
  117.9 5.4 %all-to-all-done.1 = f32[4,1,1536]{2,1,0:T(1,128)S(1)} async-done(((f32[4,1,1536]{2,1,0:T(1,128)}), f32[4,1,1536]{2,1,0:T(1,128)S(1)}, u32[]{:S(2)}, u32[]{:S(2)}) %all-to-all-start.1) | async-done | bytes 24608 | tf_op jit(solution)/shard_map/all_to_all | solution.py:43
  123.4 0.5 broadcast.125
  123.9 0.7 reduce
  124.6 0.1 reshape.141
  124.7 0.6 gather_fusion
  125.3 0.1 copy.21
  125.4 0.7 compare_select_fusion
  (6 shorter events, 0.0 us)
Async XLA Ops:
  7.2 2.2 %copy-start = (bf16[64,4096]{1,0:T(8,128)(2,1)S(1)}, bf16[64,4096]{1,0:T(8,128)(2,1)}, u32[]{:S(2)}) copy-start(bf16[64,4096]{1,0:T(8,128)(2,1)} %param.9) | copy-start | bytes 1572868
  15.7 6.5 %copy-start.2 = (bf16[8,1024]{1,0:T(8,128)(2,1)S(1)}, bf16[8,1024]{1,0:T(8,128)(2,1)}, u32[]{:S(2)}) copy-start(bf16[8,1024]{1,0:T(8,128)(2,1)} %param.7) | copy-start | bytes 49156
  15.7 53.8 %all-to-all-start = ((bf16[4,48,4096]{2,1,0:T(8,128)(2,1)}), bf16[4,48,4096]{2,1,0:T(8,128)(2,1)S(1)}, u32[]{:S(2)}, u32[]{:S(2)}) async-start(bf16[4,48,4096]{2,1,0:T(8,128)(2,1)} %bitcast.3), calls=%async_computation | async-start | bytes 3145728 | tf_op jit(solution)/shard_map/all_to_all | solution.py:37
  22.2 89.2 %reduce-scatter.4.cloned.1.call-start = ((), (), s32[]{:S(2)}) async-start(), calls=%async_computation.3 | async-start | bytes 294912
  74.4 2.3 %copy-start.1 = (bf16[256,1024]{1,0:T(8,128)(2,1)S(1)}, bf16[256,1024]{1,0:T(8,128)(2,1)}, u32[]{:S(2)}) copy-start(bf16[256,1024]{1,0:T(8,128)(2,1)} %param.8) | copy-start | bytes 1572868
  113.1 10.2 %all-to-all-start.1 = ((f32[4,1,1536]{2,1,0:T(1,128)}), f32[4,1,1536]{2,1,0:T(1,128)S(1)}, u32[]{:S(2)}, u32[]{:S(2)}) async-start(f32[4,1,1536]{2,1,0:T(1,128)} %reshape.140), calls=%async_computation.1 | async-start | bytes 49152 | tf_op jit(solution)/shard_map/all_to_all | solution.py:43
Sparse Core Ops, SparseCore 0:
  76.7 34.6 reduce-scatter.3
where the time goes:
time: 133 us
  blocking collectives  47.3 us (36%)
  waiting for transfers between devices  39.2 us (29%)
  between operations  14.1 us (11%)
  local copies, waits for them, and re-layouts  12.8 us (10%)
  starting transfers between devices  11.1 us (8%)
  matrix products  5.81 us (4%)
  other arithmetic  2.59 us (2%)
    all_gather x1, blocking collectives, local(): lax.all_gather(group_rows, 'grp', axis=0, tiled=True)  38.1 us
    unnamed x2, waiting for transfers between devices  33.8 us
    all_gather x1, blocking collectives, local(): group_rows = lax.all_gather(bin_sketch, 'mem', axis=0, tiled=True)  9.22 us
    all_to_all x1, starting transfers between devices, local(): lax.all_to_all(outgoing, 'grp', split_axis=0, concat_axis=0, tiled=True)  6.48 us
    scatter x1, local copies, waits for them, and re-layouts, local(): jnp.zeros((capacity, width_here), jnp.bfloat16).at[slot_index].set(source)  6.38 us
    all_to_all x1, waiting for transfers between devices, local(): lax.all_to_all(summed, 'grp', split_axis=0, concat_axis=0, tiled=True)  5.43 us
    dot_general x1, matrix products, local(): jnp.einsum('gsmc,sjc->gsmj', incoming, member_profile, preferred_element_...  4.81 us
    unnamed x12, local copies, waits for them, and re-layouts  4.76 us
  transfers between devices with their start and end apart: 3, of which 2 were waited for; matrix products, arithmetic and copies ran while one was open for 1% of the time, Pallas kernels for 0%

commit v1 on v0

--- a/solution.py
+++ b/solution.py
@@ -1,3 +1,4 @@
+import functools
 import jax
 import jax.numpy as jnp
 from jax import lax
@@ -7,11 +8,30 @@
 MOST = 16
 
 
+def routes_all_turn(xx, axis_key, array_axis):
+    extent = lax.psum(1, axis_key)
+    xs_all = [(rr, (rr + 1) % extent) for rr in range(extent)]
+    panels = [(rr, (rr - 1) % extent) for rr in range(extent)]
+    parts_out, taken_in = ([xx], [xx])
+    for _ in range(extent // 2):
+        parts_out.append(lax.ppermute(parts_out[-1], axis_key, xs_all))
+    for _ in range((extent - 1) // 2):
+        taken_in.append(lax.ppermute(taken_in[-1], axis_key, panels))
+    return jnp.roll(
+        jnp.concatenate([*parts_out[::-1], *taken_in[1:]], axis=array_axis),
+        shift=(lax.axis_index(axis_key) - extent // 2) * xx.shape[array_axis],
+        axis=array_axis,
+    )
+
+
+ways_close = functools.partial(routes_all_turn, axis_key="mem", array_axis=0)
+
+
 def local(
     bin_sketch, rep_sketch, bin_profile, member_profile, bin_routes, owner_slot, cluster_sizes
 ):
     coarse_scale = bin_sketch.shape[1] ** (-0.5)
-    group_rows = lax.all_gather(bin_sketch, "mem", axis=0, tiled=True)
+    group_rows = ways_close(bin_sketch)
     product = lax.dot_general(
         lax.all_gather(group_rows, "grp", axis=0, tiled=True),
         rep_sketch,

time: 133 us -> 121 us (0.910)
  blocking collectives: 47.3 us -> 15.9 us
  waiting for transfers between devices: 39.2 us -> 49.7 us
  starting transfers between devices: 11.1 us -> 19.6 us
    all_gather x1, blocking collectives: 38.1 us -> 15.9 us  [local(): lax.all_gather(group_rows, 'grp', axis=0, tiled=True)]
    all_to_all x1, waiting for transfers between devices: 0.01 us -> 20 us  [local(): lax.all_to_all(outgoing, 'grp', split_axis=0, concat_axis=0, tiled=True)]
    unnamed x2, waiting for transfers between devices: 33.8 us -> 17 us
    all_gather x1 -> x0, blocking collectives: 9.22 us -> none  [local(): group_rows = lax.all_gather(bin_sketch, 'mem', axis=0, tiled=True)]
    ppermute x0 -> x7, starting transfers between devices: none -> 8.53 us  [the longest x3 8.47 us: routes_all_turn(): taken_in.append(lax.ppermute(taken_in[-1], axis_key, panels))]
    ppermute x0 -> x7, waiting for transfers between devices: none -> 8.09 us  [the longest x4 7.42 us: routes_all_turn(): parts_out.append(lax.ppermute(parts_out[-1], axis_key, xs_all))]
    unnamed x12 -> x27, local copies, waits for them, and re-layouts: 4.76 us -> 4.81 us
  transfers between devices with their start and end apart: 3 -> 10, of which waited for: 2 -> 9; matrix products, arithmetic and copies ran while one was open for 1% -> 1% of each run, Pallas kernels for 0% -> 0%
where the time goes in v1:
time: 121 us
  waiting for transfers between devices  49.7 us (41%)
  starting transfers between devices  19.6 us (16%)
  blocking collectives  15.9 us (13%)
  between operations  14.2 us (12%)
  local copies, waits for them, and re-layouts  12.9 us (11%)
  matrix products  5.81 us (5%)
  other arithmetic  2.59 us (2%)
    all_to_all x1, waiting for transfers between devices, local(): lax.all_to_all(outgoing, 'grp', split_axis=0, concat_axis=0, tiled=True)  20 us
    unnamed x2, waiting for transfers between devices  17 us
    all_gather x1, blocking collectives, local(): lax.all_gather(group_rows, 'grp', axis=0, tiled=True)  15.9 us
    ppermute x3, starting transfers between devices, routes_all_turn(): taken_in.append(lax.ppermute(taken_in[-1], axis_key, panels))  8.47 us
    ppermute x4, waiting for transfers between devices, routes_all_turn(): parts_out.append(lax.ppermute(parts_out[-1], axis_key, xs_all))  7.42 us
    all_to_all x1, starting transfers between devices, local(): lax.all_to_all(outgoing, 'grp', split_axis=0, concat_axis=0, tiled=True)  6.48 us
    scatter x1, local copies, waits for them, and re-layouts, local(): jnp.zeros((capacity, width_here), jnp.bfloat16).at[slot_index].set(source)  6.38 us
    dot_general x1, matrix products, local(): jnp.einsum('gsmc,sjc->gsmj', incoming, member_profile, preferred_element_...  4.81 us
  transfers between devices with their start and end apart: 10, of which 9 were waited for; matrix products, arithmetic and copies ran while one was open for 1% of the time, Pallas kernels for 0%

profile of v1, /device:TPU:0, one launch (start us, length us, event | category | flops | bytes accessed | tf_op | source)
XLA Modules:
  0.0 120.8 jit_solution(14597713767743190903)
XLA Ops:
  7.2 0.0 copy-start
  7.2 0.8 copy.17
  8.0 0.1 eq.18
  8.2 0.1 fusion.12
  8.3 0.2 reduce_window_sum.11
  8.4 0.9 select_reduce_fusion.2
  9.3 0.0 copy-done
  9.3 6.4 %scatter_custom_fusion = bf16[192,4096]{1,0:T(8,128)(2,1)} fusion(s32[128]{0:T(128)S(1)} %fusion.14, bf16[64,4096]{1,0:T(8,128)(2,1)S(1)} %copy-done, s32[1024]{0:T(1024)S(1)} %pad_clamp_fusion.1, bf16[]{:T(256)} %constant.62.clone.1), kind=kCustom, calls=%fused_computation.9 | custom fusion | bytes 1572866 | tf_op jit(solution)/shard_map/scatter | solution.py:55
  15.7 0.0 copy-start.2
  15.7 6.5 %all-to-all-start = ((bf16[4,48,4096]{2,1,0:T(8,128)(2,1)}), bf16[4,48,4096]{2,1,0:T(8,128)(2,1)S(1)}, u32[]{:S(2)}, u32[]{:S(2)}) async-start(bf16[4,48,4096]{2,1,0:T(8,128)(2,1)} %bitcast.3), calls=%async_computation | async-start | bytes 3145728 | tf_op jit(solution)/shard_map/all_to_all | solution.py:57
  22.2 0.0 reduce-scatter.4.cloned.1.call-start
  22.2 0.0 copy-done.2
  22.2 0.1 collective-permute-start
  22.3 4.0 %collective-permute-done = bf16[8,1024]{1,0:T(8,128)(2,1)S(1)} collective-permute-done((bf16[8,1024]{1,0:T(8,128)(2,1)S(1)}, bf16[8,1024]{1,0:T(8,128)(2,1)S(1)}, u32[]{:S(2)}, u32[]{:S(2)}) %collective-permute-start) | collective-permute-done | bytes 16416 | tf_op jit(solution)/shard_map/ppermute | solution.py:17
  26.3 0.0 collective-permute-start.1
  26.3 2.6 %collective-permute-start.4 = (bf16[8,1024]{1,0:T(8,128)(2,1)S(1)}, bf16[8,1024]{1,0:T(8,128)(2,1)S(1)}, u32[]{:S(2)}, u32[]{:S(2)}) collective-permute-start(bf16[8,1024]{1,0:T(8,128)(2,1)S(1)} %copy-done.2), channel_id=1, source_target_pairs={{0,7},{1,0},{2,1},{3,2},{4,3},{5,4},{6,5},{7,6},{8,15},{9,8},{10,9... | collective-permute-start | bytes 49160 | tf_op jit(solution)/shard_map/ppermute | solution.py:19
  29.0 1.4 %collective-permute-done.1 = bf16[8,1024]{1,0:T(8,128)(2,1)S(1)} collective-permute-done((bf16[8,1024]{1,0:T(8,128)(2,1)S(1)}, bf16[8,1024]{1,0:T(8,128)(2,1)S(1)}, u32[]{:S(2)}, u32[]{:S(2)}) %collective-permute-start.1) | collective-permute-done | bytes 16416 | tf_op jit(solution)/shard_map/ppermute | solution.py:17
  30.4 0.0 collective-permute-start.2
  30.4 0.0 collective-permute-done.4
  30.4 2.9 %collective-permute-start.5 = (bf16[8,1024]{1,0:T(8,128)(2,1)S(1)}, bf16[8,1024]{1,0:T(8,128)(2,1)S(1)}, u32[]{:S(2)}, u32[]{:S(2)}) collective-permute-start(bf16[8,1024]{1,0:T(8,128)(2,1)S(1)} %collective-permute-done.4), channel_id=1, source_target_pairs={{0,7},{1,0},{2,1},{3,2},{4,3},{5,4},{6,5},{7,6},{8,15},{9,8},{10,9... | collective-permute-start | bytes 49160 | tf_op jit(solution)/shard_map/ppermute | solution.py:19
  33.3 1.1 collective-permute-done.2
  34.5 0.0 collective-permute-start.3
  34.5 0.1 lt.52
  34.6 0.1 copy.18
  34.7 0.1 collective-permute-done.5
  34.8 2.9 %collective-permute-start.6 = (bf16[8,1024]{1,0:T(8,128)(2,1)S(1)}, bf16[8,1024]{1,0:T(8,128)(2,1)S(1)}, u32[]{:S(2)}, u32[]{:S(2)}) collective-permute-start(bf16[8,1024]{1,0:T(8,128)(2,1)S(1)} %collective-permute-done.5), channel_id=1, source_target_pairs={{0,7},{1,0},{2,1},{3,2},{4,3},{5,4},{6,5},{7,6},{8,15},{9,8},{10,9... | collective-permute-start | bytes 49160 | tf_op jit(solution)/shard_map/ppermute | solution.py:19
  37.7 0.8 collective-permute-done.3
  38.6 0.6 collective-permute-done.6
  39.2 20.0 %all-to-all-done = bf16[4,48,4096]{2,1,0:T(8,128)(2,1)S(1)} async-done(((bf16[4,48,4096]{2,1,0:T(8,128)(2,1)}), bf16[4,48,4096]{2,1,0:T(8,128)(2,1)S(1)}, u32[]{:S(2)}, u32[]{:S(2)}) %all-to-all-start) | async-done | bytes 1572896 | tf_op jit(solution)/shard_map/all_to_all | solution.py:57
  59.2 4.8 %fusion.4 = f32[4,3,16,256]{3,2,0,1:T(8,128)S(1)} fusion(bf16[3,256,4096]{2,1,0:T(8,128)(2,1)} %param.10, bf16[4,3,16,4096]{3,2,1,0:T(8,128)(2,1)S(1)} %bitcast.25), kind=kOutput, calls=%fused_computation.8 | convolution fusion | flops 402653184 | bytes 8060928 | tf_op jit(solution)/shard_map/gsmc,sjc->gsmj/dot_general | solution.py:59
  64.0 0.7 copy.23
  64.7 0.0 copy-start.1
  64.7 1.5 %reshape.132 = f32[256,192]{1,0:T(8,128)} reshape(f32[256,3,4,16]{3,2,1,0:T(4,128)S(1)} %bitcast.24) | data formatting | bytes 393216
  66.2 0.0 reduce-scatter.4.cloned.1.call-update
  66.3 15.9 %all_gather.3 = bf16[256,1024]{1,0:T(8,128)(2,1)S(1)} all-gather(bf16[64,1024]{1,0:T(8,128)(2,1)S(1)} %constant_dynamic-slice_fusion), channel_id=1, replica_groups=mesh['grp'=4,'mem'=8] {'grp'}, dimensions={0}, use_global_device_ids=true | all-gather | bytes 655360 | tf_op jit(solution)/shard_map/all_gather | solution.py:36
  82.2 17.0 %reduce-scatter.4.cloned.1.call-done = f32[32,192]{1,0:T(8,128)} async-done(((f32[256,192]{1,0:T(8,128)}), f32[32,192]{1,0:T(8,128)}) %reduce-scatter.4.cloned.1.call-update) | async-done | bytes 24592
  99.2 0.9 reshape.133
  100.1 0.1 copy.20
  100.2 0.7 reshape.140
  100.9 4.6 %all-to-all-start.1 = ((f32[4,1,1536]{2,1,0:T(1,128)}), f32[4,1,1536]{2,1,0:T(1,128)S(1)}, u32[]{:S(2)}, u32[]{:S(2)}) async-start(f32[4,1,1536]{2,1,0:T(1,128)} %reshape.140), calls=%async_computation.1 | async-start | bytes 49152 | tf_op jit(solution)/shard_map/all_to_all | solution.py:63
  105.5 0.0 copy-done.1
  105.5 1.0 fusion.3
  106.5 4.6 %all-to-all-done.1 = f32[4,1,1536]{2,1,0:T(1,128)S(1)} async-done(((f32[4,1,1536]{2,1,0:T(1,128)}), f32[4,1,1536]{2,1,0:T(1,128)S(1)}, u32[]{:S(2)}, u32[]{:S(2)}) %all-to-all-start.1) | async-done | bytes 24608 | tf_op jit(solution)/shard_map/all_to_all | solution.py:63
  111.2 0.5 broadcast.126
  111.7 0.7 reduce
  112.4 0.1 reshape.141
  112.5 0.6 gather_fusion
  113.2 0.1 copy.21
  113.2 0.7 compare_select_fusion
  (23 shorter events, 0.1 us)
Async XLA Ops:
  7.2 2.2 %copy-start = (bf16[64,4096]{1,0:T(8,128)(2,1)S(1)}, bf16[64,4096]{1,0:T(8,128)(2,1)}, u32[]{:S(2)}) copy-start(bf16[64,4096]{1,0:T(8,128)(2,1)} %param.9) | copy-start | bytes 1572868
  15.7 6.5 %copy-start.2 = (bf16[8,1024]{1,0:T(8,128)(2,1)S(1)}, bf16[8,1024]{1,0:T(8,128)(2,1)}, u32[]{:S(2)}) copy-start(bf16[8,1024]{1,0:T(8,128)(2,1)} %param.7) | copy-start | bytes 49156
  15.7 43.4 %all-to-all-start = ((bf16[4,48,4096]{2,1,0:T(8,128)(2,1)}), bf16[4,48,4096]{2,1,0:T(8,128)(2,1)S(1)}, u32[]{:S(2)}, u32[]{:S(2)}) async-start(bf16[4,48,4096]{2,1,0:T(8,128)(2,1)} %bitcast.3), calls=%async_computation | async-start | bytes 3145728 | tf_op jit(solution)/shard_map/all_to_all | solution.py:57
  22.2 77.0 %reduce-scatter.4.cloned.1.call-start = ((), (), s32[]{:S(2)}) async-start(), calls=%async_computation.3 | async-start | bytes 294912
  22.2 4.1 %collective-permute-start = (bf16[8,1024]{1,0:T(8,128)(2,1)S(1)}, bf16[8,1024]{1,0:T(8,128)(2,1)S(1)}, u32[]{:S(2)}, u32[]{:S(2)}) collective-permute-start(bf16[8,1024]{1,0:T(8,128)(2,1)S(1)} %copy-done.2), channel_id=1, source_target_pairs={{0,1},{1,2},{2,3},{3,4},{4,5},{5,6},{6,7},{7,0},{8,9},{9,10},{10,1... | collective-permute-start | bytes 49160 | tf_op jit(solution)/shard_map/ppermute | solution.py:17
  26.3 4.1 %collective-permute-start.1 = (bf16[8,1024]{1,0:T(8,128)(2,1)S(1)}, bf16[8,1024]{1,0:T(8,128)(2,1)S(1)}, u32[]{:S(2)}, u32[]{:S(2)}) collective-permute-start(bf16[8,1024]{1,0:T(8,128)(2,1)S(1)} %collective-permute-done), channel_id=1, source_target_pairs={{0,1},{1,2},{2,3},{3,4},{4,5},{5,6},{6,7},{7,0},{8,9},{9,10},{10,1... | collective-permute-start | bytes 49160 | tf_op jit(solution)/shard_map/ppermute | solution.py:17
  26.3 4.1 %collective-permute-start.4 = (bf16[8,1024]{1,0:T(8,128)(2,1)S(1)}, bf16[8,1024]{1,0:T(8,128)(2,1)S(1)}, u32[]{:S(2)}, u32[]{:S(2)}) collective-permute-start(bf16[8,1024]{1,0:T(8,128)(2,1)S(1)} %copy-done.2), channel_id=1, source_target_pairs={{0,7},{1,0},{2,1},{3,2},{4,3},{5,4},{6,5},{7,6},{8,15},{9,8},{10,9... | collective-permute-start | bytes 49160 | tf_op jit(solution)/shard_map/ppermute | solution.py:19
  30.4 4.1 %collective-permute-start.2 = (bf16[8,1024]{1,0:T(8,128)(2,1)S(1)}, bf16[8,1024]{1,0:T(8,128)(2,1)S(1)}, u32[]{:S(2)}, u32[]{:S(2)}) collective-permute-start(bf16[8,1024]{1,0:T(8,128)(2,1)S(1)} %collective-permute-done.1), channel_id=1, source_target_pairs={{0,1},{1,2},{2,3},{3,4},{4,5},{5,6},{6,7},{7,0},{8,9},{9,10},{10,1... | collective-permute-start | bytes 49160 | tf_op jit(solution)/shard_map/ppermute | solution.py:17
  30.4 4.4 %collective-permute-start.5 = (bf16[8,1024]{1,0:T(8,128)(2,1)S(1)}, bf16[8,1024]{1,0:T(8,128)(2,1)S(1)}, u32[]{:S(2)}, u32[]{:S(2)}) collective-permute-start(bf16[8,1024]{1,0:T(8,128)(2,1)S(1)} %collective-permute-done.4), channel_id=1, source_target_pairs={{0,7},{1,0},{2,1},{3,2},{4,3},{5,4},{6,5},{7,6},{8,15},{9,8},{10,9... | collective-permute-start | bytes 49160 | tf_op jit(solution)/shard_map/ppermute | solution.py:19
  34.5 4.1 %collective-permute-start.3 = (bf16[8,1024]{1,0:T(8,128)(2,1)S(1)}, bf16[8,1024]{1,0:T(8,128)(2,1)S(1)}, u32[]{:S(2)}, u32[]{:S(2)}) collective-permute-start(bf16[8,1024]{1,0:T(8,128)(2,1)S(1)} %collective-permute-done.2), channel_id=1, source_target_pairs={{0,1},{1,2},{2,3},{3,4},{4,5},{5,6},{6,7},{7,0},{8,9},{9,10},{10,1... | collective-permute-start | bytes 49160 | tf_op jit(solution)/shard_map/ppermute | solution.py:17
  34.8 4.4 %collective-permute-start.6 = (bf16[8,1024]{1,0:T(8,128)(2,1)S(1)}, bf16[8,1024]{1,0:T(8,128)(2,1)S(1)}, u32[]{:S(2)}, u32[]{:S(2)}) collective-permute-start(bf16[8,1024]{1,0:T(8,128)(2,1)S(1)} %collective-permute-done.5), channel_id=1, source_target_pairs={{0,7},{1,0},{2,1},{3,2},{4,3},{5,4},{6,5},{7,6},{8,15},{9,8},{10,9... | collective-permute-start | bytes 49160 | tf_op jit(solution)/shard_map/ppermute | solution.py:19
  64.7 40.8 %copy-start.1 = (bf16[256,1024]{1,0:T(8,128)(2,1)S(1)}, bf16[256,1024]{1,0:T(8,128)(2,1)}, u32[]{:S(2)}) copy-start(bf16[256,1024]{1,0:T(8,128)(2,1)} %param.8) | copy-start | bytes 1572868
  100.9 10.2 %all-to-all-start.1 = ((f32[4,1,1536]{2,1,0:T(1,128)}), f32[4,1,1536]{2,1,0:T(1,128)S(1)}, u32[]{:S(2)}, u32[]{:S(2)}) async-start(f32[4,1,1536]{2,1,0:T(1,128)} %reshape.140), calls=%async_computation.1 | async-start | bytes 49152 | tf_op jit(solution)/shard_map/all_to_all | solution.py:63
Sparse Core Ops, SparseCore 0:
  66.3 32.7 reduce-scatter.3
